TPU v7x, 32 devices: a whole 2x2x4 slice. The times are simulated.
32 devices in a mesh: dp: 8 (over z, x), tensor: 4 (over y, core).
Axes of the slice: x: 2, y: 2, z: 4, core: 2. Of those that a mesh axis runs over, the one named last changes fastest.
Arguments:
- hidden_in: bfloat16 [16384, 768], P('dp'), may hold values from -6 to 6
- doc_ids: int32 [16384], P('dp'), may hold values from 0 to 7, as said below
- ln1_gain: float32 [768], replicated, may hold values from 0.5 to 1.5
- ln1_bias: float32 [768], replicated, may hold values from -1.25 to 1.25
- w_qkv: bfloat16 [768, 3, 12, 64], P(None, None, 'tensor'), may hold values from -0.3125 to 0.3125
- b_qv: float32 [2, 12, 64], P(None, 'tensor'), may hold values from -1.75 to 1.75
- w_out: bfloat16 [12, 64, 768], P('tensor'), may hold values from -0.875 to 0.875
- b_out: float32 [768], replicated, may hold values from -1.25 to 1.25
- ln2_gain: float32 [768], replicated, may hold values from 0.5 to 1.5
- ln2_bias: float32 [768], replicated, may hold values from -1.25 to 1.25
- w_fc: bfloat16 [768, 3072], P(None, 'tensor'), may hold values from -0.21875 to 0.21875
- b_fc: float32 [24, 128], P('tensor'), may hold values from -1.75 to 1.75
- w_proj: bfloat16 [3072, 768], P('tensor'), may hold values from -0.109375 to 0.109375
- b_proj: float32 [768], replicated, may hold values from -1.25 to 1.25
- grad_out: bfloat16 [16384, 768], P('dp'), may hold values from -6 to 6
Outputs:
- block_out: bfloat16 [16384, 768], P('dp')
- grad_in: float32 [16384, 768], P('dp')
- grad_ln1_gain: float32 [768], P('dp')
- grad_ln1_bias: float32 [768], P('dp')
- grad_w_qkv: float32 [768, 3, 12, 64], P('dp', None, 'tensor')
- grad_b_qv: float32 [2, 12, 64], P(None, 'tensor', 'dp')
- grad_w_out: float32 [12, 64, 768], P('tensor', None, 'dp')
- grad_b_out: float32 [768], P('dp')
- grad_ln2_gain: float32 [768], P('dp')
- grad_ln2_bias: float32 [768], P('dp')
- grad_w_fc: float32 [768, 3072], P('dp', 'tensor')
- grad_b_fc: float32 [24, 128], P('tensor', 'dp')
- grad_w_proj: float32 [3072, 768], P('tensor', 'dp')
- grad_b_proj: float32 [768], P('dp')
Inputs may be any that keep to these rules, and one draw needn't show every extreme that they name: `doc_ids`: each aligned block of 2048 tokens (one index of dp) holds either 2048 // 1024 sequences of 1024 tokens or 8 sequences of 256 tokens, numbered from 0 in order; exactly half of the blocks hold the long ones.
All inputs are finite; a program needn't handle non-finite values.
Results may differ from a plain program's by a relative error of at most 0.015.
The roundings to bfloat16 on the way count: a program that leaves them out, or rounds other values in their place, can miss the bound.
Values may be sent and summed in bfloat16 or wider, within the bound.
No kernel may reach another device: no remote copies, remote signals or barrier semaphores. Data moves between devices by JAX's collectives and lax.ppermute only.
A program may use at most 192 MiB of HBM per device.

v0:
```python
import math
import jax
import jax.numpy as jnp
from jax import lax
from jax.sharding import PartitionSpec as P

EPSILON = 1e-05
MASKED = -1e30


def normalize(values):
    row_mean = jnp.mean(values, axis=-1, keepdims=True)
    centered = values - row_mean
    inv_std = lax.rsqrt(jnp.mean(centered * centered, axis=-1, keepdims=True) + EPSILON)
    return (centered * inv_std, inv_std)


def norm_back(grad_normed, normed, inv_std, gain_vec):
    scaled = grad_normed * gain_vec
    return inv_std * (
        scaled
        - jnp.mean(scaled, axis=-1, keepdims=True)
        - normed * jnp.mean(scaled * normed, axis=-1, keepdims=True)
    )


def masked_scores(queries, key_rows, row_ids, key_ids, start_row, scale_factor):
    scores = (
        jnp.einsum("qhd,khd->hqk", queries, key_rows, preferred_element_type=jnp.float32)
        * scale_factor
    )
    row_pos = start_row + jnp.arange(queries.shape[0])
    key_pos = jnp.arange(key_rows.shape[0])
    allowed = (row_pos[:, None] >= key_pos[None, :]) & (row_ids[:, None] == key_ids[None, :])
    return jnp.where(allowed[None], scores, MASKED)


def body(
    hidden_in,
    doc_ids,
    ln1_gain,
    ln1_bias,
    w_qkv,
    b_qv,
    w_out,
    b_out,
    ln2_gain,
    ln2_bias,
    w_fc,
    b_fc,
    w_proj,
    b_proj,
    grad_out,
):
    row_count, model_width = hidden_in.shape
    local_heads = w_qkv.shape[2]
    head_dim = w_qkv.shape[3]
    local_width = local_heads * head_dim
    hidden_units = w_fc.shape[1]
    scale_factor = 1.0 / math.sqrt(head_dim)
    block_rows = min(512, row_count)
    block_count = row_count // block_rows
    qkv_matrix = w_qkv.reshape(model_width, 3 * local_width)
    out_matrix = w_out.reshape(local_width, model_width)
    x_float = hidden_in.astype(jnp.float32)
    normed_one, inv_one = normalize(x_float)
    first_in = (normed_one * ln1_gain + ln1_bias).astype(jnp.bfloat16)
    projected = jnp.dot(first_in, qkv_matrix, preferred_element_type=jnp.float32).reshape(
        row_count, 3, local_heads, head_dim
    )
    queries = (projected[:, 0] + b_qv[0]).astype(jnp.bfloat16)
    key_rows = projected[:, 1].astype(jnp.bfloat16)
    value_rows = (projected[:, 2] + b_qv[1]).astype(jnp.bfloat16)
    attended_parts = []
    log_totals = []
    for block_index in range(block_count):
        start_row = block_index * block_rows
        end_row = start_row + block_rows
        scores = masked_scores(
            queries[start_row:end_row],
            key_rows[:end_row],
            doc_ids[start_row:end_row],
            doc_ids[:end_row],
            start_row,
            scale_factor,
        )
        row_max = jnp.max(scores, axis=-1, keepdims=True)
        exp_scores = jnp.exp(scores - row_max)
        row_total = jnp.sum(exp_scores, axis=-1, keepdims=True)
        weights_low = (exp_scores / row_total).astype(jnp.bfloat16)
        log_totals.append(row_max + jnp.log(row_total))
        attended_parts.append(
            jnp.einsum(
                "hqk,khd->qhd",
                weights_low,
                value_rows[:end_row],
                preferred_element_type=jnp.float32,
            )
        )
    attended = (
        jnp.concatenate(attended_parts, axis=0).reshape(row_count, local_width).astype(jnp.bfloat16)
    )
    branch_part = jnp.dot(attended, out_matrix, preferred_element_type=jnp.float32)
    branch = lax.psum(branch_part, "tensor") + b_out
    residual = x_float + branch
    normed_two, inv_two = normalize(residual)
    second_in = (normed_two * ln2_gain + ln2_bias).astype(jnp.bfloat16)
    pre_act = jnp.dot(second_in, w_fc, preferred_element_type=jnp.float32) + b_fc.reshape(
        hidden_units
    )
    act_value, gelu_back = jax.vjp(
        lambda pre_value: jax.nn.gelu(pre_value, approximate=True), pre_act
    )
    act_low = act_value.astype(jnp.bfloat16)
    mlp_part = jnp.dot(act_low, w_proj, preferred_element_type=jnp.float32)
    block_out = (
        residual + lax.psum(mlp_part.astype(jnp.bfloat16), "tensor").astype(jnp.float32) + b_proj
    )
    grad_float = grad_out.astype(jnp.float32)
    grad_w_proj = jnp.einsum("rf,rd->fd", act_low, grad_out, preferred_element_type=jnp.float32)
    grad_b_proj = jnp.sum(grad_float, axis=0)
    grad_act = jnp.einsum("rd,fd->rf", grad_out, w_proj, preferred_element_type=jnp.float32)
    grad_pre = gelu_back(grad_act)[0].astype(jnp.bfloat16)
    grad_w_fc = jnp.einsum("rd,rf->df", second_in, grad_pre, preferred_element_type=jnp.float32)
    grad_b_fc = jnp.sum(grad_pre.astype(jnp.float32), axis=0).reshape(b_fc.shape)
    grad_second_part = jnp.einsum("rf,df->rd", grad_pre, w_fc, preferred_element_type=jnp.float32)
    grad_second = lax.psum(grad_second_part, "tensor")
    grad_ln2_gain = jnp.sum(grad_second * normed_two, axis=0)
    grad_ln2_bias = jnp.sum(grad_second, axis=0)
    grad_residual = grad_float + norm_back(grad_second, normed_two, inv_two, ln2_gain)
    grad_branch = grad_residual.astype(jnp.bfloat16)
    grad_b_out = jnp.sum(grad_branch.astype(jnp.float32), axis=0)
    grad_w_out = jnp.einsum(
        "rc,rd->cd", attended, grad_branch, preferred_element_type=jnp.float32
    ).reshape(w_out.shape)
    grad_attended = (
        jnp.einsum("rd,cd->rc", grad_branch, out_matrix, preferred_element_type=jnp.float32)
        .astype(jnp.bfloat16)
        .reshape(row_count, local_heads, head_dim)
    )
    grad_query_parts = []
    grad_keys = jnp.zeros((row_count, local_heads, head_dim), jnp.float32)
    grad_values = jnp.zeros((row_count, local_heads, head_dim), jnp.float32)
    for block_index in range(block_count):
        start_row = block_index * block_rows
        end_row = start_row + block_rows
        block_queries = queries[start_row:end_row]
        scores = masked_scores(
            block_queries,
            key_rows[:end_row],
            doc_ids[start_row:end_row],
            doc_ids[:end_row],
            start_row,
            scale_factor,
        )
        attn_weights = jnp.exp(scores - log_totals[block_index])
        weights_low = attn_weights.astype(jnp.bfloat16)
        grad_rows = grad_attended[start_row:end_row]
        grad_weights = jnp.einsum(
            "qhd,khd->hqk", grad_rows, value_rows[:end_row], preferred_element_type=jnp.float32
        )
        row_delta = jnp.sum(attn_weights * grad_weights, axis=-1, keepdims=True)
        grad_scores = (attn_weights * (grad_weights - row_delta)).astype(jnp.bfloat16)
        grad_query_parts.append(
            jnp.einsum(
                "hqk,khd->qhd", grad_scores, key_rows[:end_row], preferred_element_type=jnp.float32
            )
            * scale_factor
        )
        grad_keys = grad_keys.at[:end_row].add(
            jnp.einsum(
                "hqk,qhd->khd", grad_scores, block_queries, preferred_element_type=jnp.float32
            )
            * scale_factor
        )
        grad_values = grad_values.at[:end_row].add(
            jnp.einsum("hqk,qhd->khd", weights_low, grad_rows, preferred_element_type=jnp.float32)
        )
    grad_queries = jnp.concatenate(grad_query_parts, axis=0)
    grad_mixed = jnp.stack([grad_queries, grad_keys, grad_values], axis=1).astype(jnp.bfloat16)
    grad_flat = grad_mixed.reshape(row_count, 3 * local_width)
    grad_w_qkv = jnp.einsum(
        "rd,rc->dc", first_in, grad_flat, preferred_element_type=jnp.float32
    ).reshape(w_qkv.shape)
    grad_b_qv = jnp.stack(
        [
            jnp.sum(grad_mixed[:, 0].astype(jnp.float32), axis=0),
            jnp.sum(grad_mixed[:, 2].astype(jnp.float32), axis=0),
        ],
        axis=0,
    )
    grad_first_part = jnp.einsum(
        "rc,dc->rd", grad_flat, qkv_matrix, preferred_element_type=jnp.float32
    )
    grad_first = lax.psum(grad_first_part.astype(jnp.bfloat16), "tensor").astype(jnp.float32)
    grad_ln1_gain = jnp.sum(grad_first * normed_one, axis=0)
    grad_ln1_bias = jnp.sum(grad_first, axis=0)
    grad_in = grad_residual + norm_back(grad_first, normed_one, inv_one, ln1_gain)
    shares = (
        lax.psum_scatter(grad_ln1_gain, "dp", scatter_dimension=0, tiled=True),
        lax.psum_scatter(grad_ln1_bias, "dp", scatter_dimension=0, tiled=True),
        lax.psum_scatter(grad_w_qkv, "dp", scatter_dimension=0, tiled=True),
        lax.psum_scatter(grad_b_qv, "dp", scatter_dimension=2, tiled=True),
        lax.psum_scatter(grad_w_out, "dp", scatter_dimension=2, tiled=True),
        lax.psum_scatter(grad_b_out, "dp", scatter_dimension=0, tiled=True),
        lax.psum_scatter(grad_ln2_gain, "dp", scatter_dimension=0, tiled=True),
        lax.psum_scatter(grad_ln2_bias, "dp", scatter_dimension=0, tiled=True),
        lax.psum_scatter(grad_w_fc, "dp", scatter_dimension=0, tiled=True),
        lax.psum_scatter(grad_b_fc, "dp", scatter_dimension=1, tiled=True),
        lax.psum_scatter(grad_w_proj, "dp", scatter_dimension=1, tiled=True),
        lax.psum_scatter(grad_b_proj, "dp", scatter_dimension=0, tiled=True),
    )
    return (
        block_out.astype(jnp.bfloat16),
        grad_in,
        shares[0],
        shares[1],
        shares[2],
        shares[3],
        shares[4],
        shares[5],
        shares[6],
        shares[7],
        shares[8],
        shares[9],
        shares[10],
        shares[11],
    )


def solution(mesh):
    in_specs = (
        P("dp", None),
        P("dp"),
        P(),
        P(),
        P(None, None, "tensor", None),
        P(None, "tensor", None),
        P("tensor", None, None),
        P(),
        P(),
        P(),
        P(None, "tensor"),
        P("tensor", None),
        P("tensor", None),
        P(),
        P("dp", None),
    )
    out_specs = (
        P("dp", None),
        P("dp", None),
        P("dp"),
        P("dp"),
        P("dp", None, "tensor", None),
        P(None, "tensor", "dp"),
        P("tensor", None, "dp"),
        P("dp"),
        P("dp"),
        P("dp"),
        P("dp", "tensor"),
        P("tensor", "dp"),
        P("tensor", "dp"),
        P("dp"),
    )
    return jax.shard_map(body, mesh=mesh, in_specs=in_specs, out_specs=out_specs, check_vma=False)
```

profile of v0, /device:TPU:0, one launch (start us, length us, event | category | flops | bytes accessed | tf_op | source)
XLA Modules:
  0.0 799.8 jit_solution(18134782078654954278)
XLA Ops:
  9.3 2.4 convert_reduce_fusion.1
  11.7 2.9 fusion.16
  15.5 2.3 fusion.136
  25.2 2.3 fusion.138
  28.9 2.3 fusion.94
  32.2 3.8 fusion.137
  36.1 1.9 fusion
  38.0 2.6 copy-done.2
  40.6 3.1 fusion.104
  43.7 3.7 convolution_bitcast_fusion
  47.9 122.0 %all-reduce.15.cloned.1.call-done = f32[2048,768]{1,0:T(8,128)} async-done(((f32[2048,768]{1,0:T(8,128)}), f32[2048,768]{1,0:T(8,128)}) %all-reduce.15.cloned.1.call-update) | async-done | bytes 6291472 | tf_op jit(solution)/shard_map/psum | solution.py:104
  170.0 4.6 fusion.132
  177.6 2.6 fusion.141
  180.7 7.7 convert_reduce_fusion.3
  190.0 4.5 fusion.142
  195.4 6.2 convolution_convert_fusion
  201.8 112.7 %all-reduce.17.cloned.1.call-done = f32[2048,768]{1,0:T(8,128)} async-done(((f32[2048,768]{1,0:T(8,128)}), f32[2048,768]{1,0:T(8,128)}) %all-reduce.17.cloned.1.call-update) | async-done | bytes 6291472 | tf_op jit(solution)/shard_map/psum | solution.py:127
  314.5 6.6 multiply_reduce_fusion.2
  321.8 5.8 convert_reduce_fusion.4
  327.7 2.1 fusion.40
  332.5 2.3 multiply_reduce_fusion.7
  335.0 4.2 multiply_reduce_fusion.3
  341.1 5.7 multiply_reduce_fusion.1
  346.8 2.1 fusion.61
  349.1 6.4 multiply_reduce_fusion
  355.6 3.1 fusion.67
  358.7 2.9 multiply_convert_fusion.4
  362.8 3.5 multiply_convert_fusion.2
  366.3 2.1 fusion.101
  369.2 5.4 multiply_convert_fusion.1
  377.1 6.3 multiply_convert_fusion
  383.4 2.0 fusion.99
  385.5 2.1 fusion.57
  393.6 5.5 bitcast_convert_fusion
  399.8 5.5 fusion.71
  405.3 2.8 copy.57
  408.2 6.9 fusion.143
  415.2 6.9 fusion.144
  425.8 29.0 %reduce-scatter.19.cloned.1.call-done = f32[96,192]{1,0:T(8,128)} async-done(((f32[768,192]{1,0:T(8,128)}), f32[96,192]{1,0:T(8,128)}) %reduce-scatter.19.cloned.1.call-update) | async-done | bytes 73744
  456.5 119.1 %all-reduce.19.cloned.1.call-done = (bf16[2048,768]{1,0:T(8,128)(2,1)}, bf16[2048,768]{1,0:T(8,128)(2,1)}) async-done(((bf16[2048,768]{1,0:T(8,128)(2,1)}, bf16[2048,768]{1,0:T(8,128)(2,1)}), (bf16[2048,768]{1,0:T(8,128)(2,1)}, bf16[2048,768]{1,0:T(8,128)(2,1)})) %all-reduce.19.cloned.1.call-update) | async-done | bytes 6291472 | tf_op jit(solution)/shard_map/psum | solution.py:117
  575.6 5.2 fusion.25
  580.9 38.1 %all-reduce.9 = (f32[768]{0:T(1024)S(1)}, f32[768]{0:T(1024)S(1)}, f32[2,3,64]{2,1,0:T(4,128)S(1)}, f32[768]{0:T(1024)S(1)}, f32[768]{0:T(1024)S(1)}, /*index=5*/f32[768]{0:T(1024)S(1)}, f32[768]{0:T(1024)S(1)}) all-reduce(f32[768]{0:T(1024)S(1)} %get-tuple-element.156, ...), channel_id=2, replica_groups=mesh['dp'=8,'tensor'=4] {'dp'}, use_global_device_ids=true, to_apply=%region_25.26.clone | all-reduce | flops 4992 | bytes 39936
  623.2 6.4 add_convert_fusion
  631.2 4.2 fusion.15
  635.4 11.5 %reduce-scatter.17.cloned.1.call-done = f32[96,576]{1,0:T(8,128)} async-done(((f32[768,576]{1,0:T(8,128)}), f32[96,576]{1,0:T(8,128)}) %reduce-scatter.17.cloned.1.call-update) | async-done | bytes 221200
  647.0 1.8 copy.58
  648.8 70.8 %reduce-scatter.13.cloned.1.call-done = f32[96,768]{1,0:T(8,128)} async-done(((f32[768,768]{1,0:T(8,128)}), f32[96,768]{1,0:T(8,128)}) %reduce-scatter.13.cloned.1.call-update) | async-done | bytes 294928 | tf_op jit(solution)/shard_map/reduce_scatter | solution.py:208
  719.6 72.9 %reduce-scatter.15.cloned.1.call-done = f32[768,96]{0,1:T(8,128)} async-done(((f32[768,768]{0,1:T(8,128)}), f32[768,96]{0,1:T(8,128)}) %reduce-scatter.15.cloned.1.call-update) | async-done | bytes 294928 | tf_op jit(solution)/shard_map/reduce_scatter | solution.py:210
  (198 shorter events, 45.7 us)
Async XLA Ops:
  7.2 173.1 %copy-start = (bf16[768,768]{1,0:T(8,128)(2,1)S(1)}, bf16[768,768]{1,0:T(8,128)(2,1)}, u32[]{:S(2)}) copy-start(bf16[768,768]{1,0:T(8,128)(2,1)} %param.47) | copy-start | bytes 3538948
  7.2 7.7 slice-start.12
  7.2 8.2 %copy-start.33 = (f32[768]{0:T(1024)S(1)}, f32[768]{0:T(1024)}, u32[]{:S(2)}) copy-start(f32[768]{0:T(1024)} %param.37) | copy-start | bytes 9220
  7.2 8.2 %copy-start.39 = (bf16[768,3,3,64]{0,3,2,1:T(8,128)(2,1)S(1)}, bf16[768,3,3,64]{0,3,2,1:T(8,128)(2,1)}, u32[]{:S(2)}) copy-start(bf16[768,3,3,64]{0,3,2,1:T(8,128)(2,1)} %param.39) | copy-start | bytes 2654212
  7.2 8.2 %copy-start.41 = (f32[768]{0:T(1024)S(1)}, f32[768]{0:T(1024)}, u32[]{:S(2)}) copy-start(f32[768]{0:T(1024)} %param.38) | copy-start | bytes 9220
  7.2 162.7 %all-reduce.15.cloned.1.call-start = ((), (), s32[]{:S(2)}) async-start(), calls=%async_computation.5 | async-start | bytes 12582912 | tf_op jit(solution)/shard_map/psum | solution.py:104
  7.3 8.2 %copy-start.7 = (bf16[2048,768]{1,0:T(8,128)(2,1)S(1)}, bf16[2048,768]{1,0:T(8,128)(2,1)}, u32[]{:S(2)}) copy-start(bf16[2048,768]{1,0:T(8,128)(2,1)} %param.35) | copy-start | bytes 9437188
  11.7 6.1 copy-start.23
  14.7 3.1 copy-start.26
  17.8 7.4 copy-start.20
  18.0 14.2 %copy-start.13 = (bf16[2048,3,64]{0,2,1:T(8,128)(2,1)}, bf16[2048,3,64]{0,2,1:T(8,128)(2,1)S(1)}, u32[]{:S(2)}) copy-start(bf16[2048,3,64]{0,2,1:T(8,128)(2,1)S(1)} %get-tuple-element.180) | copy-start | bytes 2359300
  27.5 3.7 copy-start.4
  36.1 4.5 copy-start.2
  40.6 3.1 copy-start.22
  43.7 126.2 %copy-start.37 = (f32[768]{0:T(1024)S(1)}, f32[768]{0:T(1024)}, u32[]{:S(2)}) copy-start(f32[768]{0:T(1024)} %param.42) | copy-start | bytes 9220
  47.5 267.0 %all-reduce.17.cloned.1.call-start = ((), (), s32[]{:S(2)}) async-start(), calls=%async_computation.6 | async-start | bytes 12582912 | tf_op jit(solution)/shard_map/psum | solution.py:127
  177.6 3.0 copy-start.18
  177.6 3.0 copy-start.40
  194.5 229.6 %reduce-scatter.21.cloned.1.call-start = ((), (), s32[]{:S(2)}) async-start(), calls=%async_computation.11 | async-start | bytes 73728
  201.6 253.1 %reduce-scatter.19.cloned.1.call-start = ((), (), s32[]{:S(2)}) async-start(), calls=%async_computation.10 | async-start | bytes 884736
  314.5 6.6 copy-start.11
  314.5 7.4 copy-start.19
  327.7 3.3 copy-start.6
  331.1 3.9 slice-start.6
  335.0 5.4 slice-start.3
  335.0 5.8 slice-start.4
  341.1 7.8 slice-start
  341.1 7.8 slice-start.1
  358.7 3.7 slice-start.8
  358.7 4.1 slice-start.9
  369.2 5.4 copy-start.21
  385.5 3.2 copy-start.15
  387.6 4.6 copy-start.16
  391.1 184.6 %all-reduce.19.cloned.1.call-start = ((), (), s32[]{:S(2)}) async-start(), calls=%async_computation.12 | async-start | bytes 12582912 | tf_op jit(solution)/shard_map/psum | solution.py:117
  399.1 247.9 %reduce-scatter.17.cloned.1.call-start = ((), (), s32[]{:S(2)}) async-start(), calls=%async_computation.9 | async-start | bytes 2211840
  408.1 311.4 %reduce-scatter.13.cloned.1.call-start = ((), (), s32[]{:S(2)}) async-start(), calls=%async_computation.7 | async-start | bytes 2654208 | tf_op jit(solution)/shard_map/reduce_scatter | solution.py:208
  415.1 7.0 copy-start.43
  415.2 377.4 %reduce-scatter.15.cloned.1.call-start = ((), (), s32[]{:S(2)}) async-start(), calls=%async_computation.8 | async-start | bytes 2654208 | tf_op jit(solution)/shard_map/reduce_scatter | solution.py:210
  422.1 158.7 %copy-start.29 = (f32[768]{0:T(1024)S(1)}, f32[768]{0:T(1024)}, u32[]{:S(2)}) copy-start(f32[768]{0:T(1024)} %get-tuple-element.154) | copy-start | bytes 9220
  422.1 158.7 %copy-start.30 = (f32[768]{0:T(1024)S(1)}, f32[768]{0:T(1024)}, u32[]{:S(2)}) copy-start(f32[768]{0:T(1024)} %get-tuple-element.159) | copy-start | bytes 9220
  422.1 158.7 %copy-start.31 = (f32[768]{0:T(1024)S(1)}, f32[768]{0:T(1024)}, u32[]{:S(2)}) copy-start(f32[768]{0:T(1024)} %get-tuple-element.175) | copy-start | bytes 9220
  422.1 158.7 %copy-start.32 = (f32[768]{0:T(1024)S(1)}, f32[768]{0:T(1024)}, u32[]{:S(2)}) copy-start(f32[768]{0:T(1024)} %get-tuple-element.182) | copy-start | bytes 9220
  575.6 54.0 %slice-start.10 = ((s8[6291456]{0:T(1024)(128)(4,1)}), s8[2097152]{0:T(1024)(128)(4,1)S(1)}, s32[]{:S(2)}) async-start(s8[6291456]{0:T(1024)(128)(4,1)} %bitcast.204), calls=%async_computation.23 | async-start | bytes 4194304
  623.2 6.5 slice-start.11
  623.2 6.5 copy-start.8
  623.2 8.0 %copy-start.12 = (bf16[2048,768]{1,0:T(8,128)(2,1)S(1)}, bf16[2048,768]{1,0:T(8,128)(2,1)}, u32[]{:S(2)}) copy-start(bf16[2048,768]{1,0:T(8,128)(2,1)} %get-tuple-element.172) | copy-start | bytes 9437188
  623.2 8.0 %copy-start.35 = (f32[768]{0:T(1024)S(1)}, f32[768]{0:T(1024)}, u32[]{:S(2)}) copy-start(f32[768]{0:T(1024)} %param.37) | copy-start | bytes 9220
  623.2 169.3 %copy-start.1 = (bf16[768,768]{1,0:T(8,128)(2,1)S(1)}, bf16[768,768]{1,0:T(8,128)(2,1)}, u32[]{:S(2)}) copy-start(bf16[768,768]{1,0:T(8,128)(2,1)} %param.47) | copy-start | bytes 3538948
  (18 other events, 32.2 us)
Sparse Core Ops, SparseCore 0:
  47.6 122.2 all-reduce.14
  194.7 119.7 all-reduce.16
  318.5 62.7 reduce-scatter.20
  391.2 63.4 reduce-scatter.18
  457.0 118.6 all-reduce.18
  579.0 67.9 reduce-scatter.16
  651.0 68.4 reduce-scatter.12
  723.6 68.8 reduce-scatter.14
where the time goes:
time: 809 us; the launch traced here: 800 us
  waiting for transfers between devices  538 us (67%)
  matrix products  108 us (13%)
  other arithmetic  70 us (9%)
  blocking collectives  38.1 us (5%)
  local copies, waits for them, and re-layouts  27.9 us (3%)
  between operations  16.8 us (2%)
    psum x1, waiting for transfers between devices, body(): branch = lax.psum(branch_part, 'tensor') + b_out  122 us
    psum x1, waiting for transfers between devices, body(): lax.psum(mlp_part.astype(jnp.bfloat16), 'tensor').astype(jnp.float32)  119 us
    psum x1, waiting for transfers between devices, body(): grad_second = lax.psum(grad_second_part, 'tensor')  113 us
    reduce_scatter x1, waiting for transfers between devices, body(): lax.psum_scatter(grad_w_proj, 'dp', scatter_dimension=1, tiled=True)  72.9 us
    reduce_scatter x1, waiting for transfers between devices, body(): lax.psum_scatter(grad_w_fc, 'dp', scatter_dimension=0, tiled=True)  70.8 us
    unnamed x11, waiting for transfers between devices  40.6 us
    unnamed x1, blocking collectives  38.1 us
    unnamed x132, local copies, waits for them, and re-layouts  26.4 us
  transfers between devices with their start and end apart: 8, of which 7 were waited for; matrix products, arithmetic and copies ran while one was open for 17% of the time, Pallas kernels for 0%

commit v1 on v0

--- a/solution.py
+++ b/solution.py
@@ -124,7 +124,10 @@
     grad_w_fc = jnp.einsum("rd,rf->df", second_in, grad_pre, preferred_element_type=jnp.float32)
     grad_b_fc = jnp.sum(grad_pre.astype(jnp.float32), axis=0).reshape(b_fc.shape)
     grad_second_part = jnp.einsum("rf,df->rd", grad_pre, w_fc, preferred_element_type=jnp.float32)
-    grad_second = lax.psum(grad_second_part, "tensor")
+    size, grad_second = (lax.axis_size("tensor"), grad_second_part)
+    for far in [1 << k for k in range(size.bit_length() - 1)]:
+        pairs = [(i, i ^ far) for i in range(size)]
+        grad_second = grad_second + lax.ppermute(grad_second, "tensor", pairs)
     grad_ln2_gain = jnp.sum(grad_second * normed_two, axis=0)
     grad_ln2_bias = jnp.sum(grad_second, axis=0)
     grad_residual = grad_float + norm_back(grad_second, normed_two, inv_two, ln2_gain)

time: 809 us -> 837 us (1.035)
  waiting for transfers between devices: 538 us -> 565 us
    ppermute x0 -> x2, waiting for transfers between devices: none -> 140 us  [body(): grad_second = grad_second + lax.ppermute(grad_second, 'tensor', pairs)]
    psum x1 -> x0, waiting for transfers between devices: 113 us -> none  [body(): grad_second = lax.psum(grad_second_part, 'tensor')]
    unnamed x132 -> x134, local copies, waits for them, and re-layouts: 26.4 us -> 25.4 us
    unnamed x11 -> x10, waiting for transfers between devices: 40.6 us -> 40.6 us
  transfers between devices with their start and end apart: 8 -> 9, of which waited for: 7 -> 8; matrix products, arithmetic and copies ran while one was open for 17% -> 16% of each run, Pallas kernels for 0% -> 0%
where the time goes in v1:
time: 837 us; the launch traced here: 828 us
  waiting for transfers between devices  565 us (68%)
  matrix products  106 us (13%)
  other arithmetic  73.4 us (9%)
  blocking collectives  37.9 us (5%)
  local copies, waits for them, and re-layouts  26.9 us (3%)
  between operations  16.6 us (2%)
    ppermute x2, waiting for transfers between devices, body(): grad_second = grad_second + lax.ppermute(grad_second, 'tensor', pairs)  140 us
    psum x1, waiting for transfers between devices, body(): branch = lax.psum(branch_part, 'tensor') + b_out  122 us
    psum x1, waiting for transfers between devices, body(): lax.psum(mlp_part.astype(jnp.bfloat16), 'tensor').astype(jnp.float32)  119 us
    reduce_scatter x1, waiting for transfers between devices, body(): lax.psum_scatter(grad_w_proj, 'dp', scatter_dimension=1, tiled=True)  73 us
    reduce_scatter x1, waiting for transfers between devices, body(): lax.psum_scatter(grad_w_fc, 'dp', scatter_dimension=0, tiled=True)  70.5 us
    unnamed x10, waiting for transfers between devices  40.6 us
    unnamed x1, blocking collectives  37.9 us
    unnamed x134, local copies, waits for them, and re-layouts  25.4 us
  transfers between devices with their start and end apart: 9, of which 8 were waited for; matrix products, arithmetic and copies ran while one was open for 16% of the time, Pallas kernels for 0%

profile of v1, /device:TPU:0, one launch (start us, length us, event | category | flops | bytes accessed | tf_op | source)
XLA Modules:
  0.0 828.0 jit_solution(12516186542782562170)
XLA Ops:
  9.3 2.4 convert_reduce_fusion.1
  11.7 2.9 fusion.16
  15.5 2.3 fusion.136
  25.2 2.3 fusion.138
  28.9 2.3 fusion.94
  32.3 3.8 fusion.137
  38.1 2.6 copy-done.2
  40.7 3.1 fusion.104
  43.8 3.7 convolution_bitcast_fusion
  48.1 121.9 %all-reduce.14.cloned.1.call-done = f32[2048,768]{1,0:T(8,128)} async-done(((f32[2048,768]{1,0:T(8,128)}), f32[2048,768]{1,0:T(8,128)}) %all-reduce.14.cloned.1.call-update) | async-done | bytes 6291472 | tf_op jit(solution)/shard_map/psum | solution.py:104
  170.0 4.6 fusion.132
  177.7 2.7 fusion.141
  180.7 7.7 convert_reduce_fusion.3
  190.0 2.6 fusion.142
  192.8 10.1 %collective-permute-done = f32[2048,768]{1,0:T(8,128)S(1)} collective-permute-done((f32[2048,768]{1,0:T(8,128)S(1)}, f32[2048,768]{1,0:T(8,128)S(1)}, u32[]{:S(2)}, u32[]{:S(2)}) %collective-permute-start) | collective-permute-done | bytes 6291488 | tf_op jit(solution)/shard_map/ppermute | solution.py:130
  202.9 3.5 add.277
  208.0 6.3 convolution_convert_fusion
  214.4 129.9 %collective-permute-done.1 = f32[2048,768]{1,0:T(8,128)} collective-permute-done((f32[2048,768]{1,0:T(8,128)}, f32[2048,768]{1,0:T(8,128)}, u32[]{:S(2)}, u32[]{:S(2)}) %collective-permute-start.1) | collective-permute-done | bytes 6291488 | tf_op jit(solution)/shard_map/ppermute | solution.py:130
  344.3 8.7 %multiply_reduce_fusion.2 = (f32[768]{0:T(1024)}, f32[2048]{0:T(1024)S(1)}, f32[2048]{0:T(1024)S(1)}, f32[768]{0:T(1024)}, f32[2048,768]{1,0:T(8,128)S(1)}) fusion(f32[2048,768]{1,0:T(8,128)} %copy-done.3, f32[2048]{0:T(1024)S(1)} %add_rsqrt_fusion, f32[2048]{0:T(1024)S(1)} %broadcast_multiply_fusion.4, f32[768]{0:T(1024)S(1)} %copy-done.27, ...), kind=kLoop, calls=%fused_computation.51 | loop fusion | flops 15723008 | bytes 25207808 | tf_op jit(solution)/shard_map/reduce_sum | solution.py:131
  353.0 3.7 convert_reduce_fusion.4
  356.7 2.2 fusion.40
  361.5 2.3 multiply_reduce_fusion.7
  364.0 4.1 multiply_reduce_fusion.3
  370.1 5.7 multiply_reduce_fusion.1
  375.7 2.1 fusion.61
  378.0 6.4 multiply_reduce_fusion
  384.5 3.1 fusion.67
  387.6 2.9 multiply_convert_fusion.4
  391.6 3.5 multiply_convert_fusion.2
  395.2 2.1 fusion.101
  398.0 5.4 multiply_convert_fusion.1
  405.9 6.3 multiply_convert_fusion
  412.2 2.0 fusion.99
  414.3 2.1 fusion.57
  422.3 5.7 bitcast_convert_fusion
  428.7 5.5 fusion.71
  434.2 2.8 copy.57
  437.1 6.9 fusion.143
  444.1 6.9 fusion.144
  454.7 28.9 %reduce-scatter.19.cloned.1.call-done = f32[96,192]{1,0:T(8,128)} async-done(((f32[768,192]{1,0:T(8,128)}), f32[96,192]{1,0:T(8,128)}) %reduce-scatter.19.cloned.1.call-update) | async-done | bytes 73744
  485.3 119.2 %all-reduce.16.cloned.1.call-done = (bf16[2048,768]{1,0:T(8,128)(2,1)}, bf16[2048,768]{1,0:T(8,128)(2,1)}) async-done(((bf16[2048,768]{1,0:T(8,128)(2,1)}, bf16[2048,768]{1,0:T(8,128)(2,1)}), (bf16[2048,768]{1,0:T(8,128)(2,1)}, bf16[2048,768]{1,0:T(8,128)(2,1)})) %all-reduce.16.cloned.1.call-update) | async-done | bytes 6291472 | tf_op jit(solution)/shard_map/psum | solution.py:117
  604.5 5.2 fusion.25
  609.7 37.9 %all-reduce.9 = (f32[768]{0:T(1024)S(1)}, f32[768]{0:T(1024)S(1)}, f32[2,3,64]{2,1,0:T(4,128)S(1)}, f32[768]{0:T(1024)S(1)}, f32[768]{0:T(1024)S(1)}, /*index=5*/f32[768]{0:T(1024)S(1)}, f32[768]{0:T(1024)S(1)}) all-reduce(f32[768]{0:T(1024)S(1)} %get-tuple-element.156, ...), channel_id=2, replica_groups=mesh['dp'=8,'tensor'=4] {'dp'}, use_global_device_ids=true, to_apply=%region_24.25.clone | all-reduce | flops 4992 | bytes 39936
  651.8 6.4 add_convert_fusion
  659.8 4.2 fusion.15
  664.0 11.6 %reduce-scatter.17.cloned.1.call-done = f32[96,576]{1,0:T(8,128)} async-done(((f32[768,576]{1,0:T(8,128)}), f32[96,576]{1,0:T(8,128)}) %reduce-scatter.17.cloned.1.call-update) | async-done | bytes 221200
  677.4 70.5 %reduce-scatter.13.cloned.1.call-done = f32[96,768]{1,0:T(8,128)} async-done(((f32[768,768]{1,0:T(8,128)}), f32[96,768]{1,0:T(8,128)}) %reduce-scatter.13.cloned.1.call-update) | async-done | bytes 294928 | tf_op jit(solution)/shard_map/reduce_scatter | solution.py:211
  747.9 73.0 %reduce-scatter.15.cloned.1.call-done = f32[768,96]{0,1:T(8,128)} async-done(((f32[768,768]{0,1:T(8,128)}), f32[768,96]{0,1:T(8,128)}) %reduce-scatter.15.cloned.1.call-update) | async-done | bytes 294928 | tf_op jit(solution)/shard_map/reduce_scatter | solution.py:213
  (203 shorter events, 49.2 us)
Async XLA Ops:
  7.2 173.2 %copy-start = (bf16[768,768]{1,0:T(8,128)(2,1)S(1)}, bf16[768,768]{1,0:T(8,128)(2,1)}, u32[]{:S(2)}) copy-start(bf16[768,768]{1,0:T(8,128)(2,1)} %param.47) | copy-start | bytes 3538948
  7.2 7.7 slice-start.14
  7.2 8.2 copy-start.32
  7.2 8.2 copy-start.38
  7.2 8.2 copy-start.40
  7.2 162.8 %all-reduce.14.cloned.1.call-start = ((), (), s32[]{:S(2)}) async-start(), calls=%async_computation.5 | async-start | bytes 12582912 | tf_op jit(solution)/shard_map/psum | solution.py:104
  7.3 8.2 copy-start.7
  11.7 6.1 copy-start.22
  14.7 3.1 copy-start.25
  17.8 7.4 copy-start.19
  18.0 14.3 %copy-start.12 = (bf16[2048,3,64]{0,2,1:T(8,128)(2,1)}, bf16[2048,3,64]{0,2,1:T(8,128)(2,1)S(1)}, u32[]{:S(2)}) copy-start(bf16[2048,3,64]{0,2,1:T(8,128)(2,1)S(1)} %get-tuple-element.181) | copy-start | bytes 2359300
  27.5 3.7 copy-start.4
  36.1 4.5 copy-start.2
  40.7 3.1 copy-start.21
  43.8 126.2 %copy-start.36 = (f32[768]{0:T(1024)S(1)}, f32[768]{0:T(1024)}, u32[]{:S(2)}) copy-start(f32[768]{0:T(1024)} %param.42) | copy-start | bytes 9220
  47.5 405.5 %reduce-scatter.21.cloned.1.call-start = ((), (), s32[]{:S(2)}) async-start(), calls=%async_computation.10 | async-start | bytes 73728
  192.7 10.2 %collective-permute-start = (f32[2048,768]{1,0:T(8,128)S(1)}, f32[2048,768]{1,0:T(8,128)S(1)}, u32[]{:S(2)}, u32[]{:S(2)}) collective-permute-start(f32[2048,768]{1,0:T(8,128)S(1)} %fusion.142), channel_id=1, source_target_pairs={{0,1},{1,0},{2,3},{3,2},{4,5},{5,4},{6,7},{7,6},{8,9},{9,8},{10,11... | collective-permute-start | bytes 18874376 | tf_op jit(solution)/shard_map/ppermute | solution.py:130
  206.4 137.9 %collective-permute-start.1 = (f32[2048,768]{1,0:T(8,128)}, f32[2048,768]{1,0:T(8,128)}, u32[]{:S(2)}, u32[]{:S(2)}) collective-permute-start(f32[2048,768]{1,0:T(8,128)} %add.277), channel_id=1, source_target_pairs={{0,2},{1,3},{2,0},{3,1},{4,6},{5,7},{6,4},{7,5},{8,10},{9,11},{10,... | collective-permute-start | bytes 18874376 | tf_op jit(solution)/shard_map/ppermute | solution.py:130
  207.8 275.8 %reduce-scatter.19.cloned.1.call-start = ((), (), s32[]{:S(2)}) async-start(), calls=%async_computation.9 | async-start | bytes 884736
  208.0 145.0 %slice-start.3 = ((s8[6291456]{0:T(1024)(128)(4,1)}), s8[4194304]{0:T(1024)(128)(4,1)S(1)}, s32[]{:S(2)}) async-start(s8[6291456]{0:T(1024)(128)(4,1)} %bitcast.198), calls=%async_computation.15 | async-start | bytes 8388608
  214.4 138.6 %slice-start.4 = ((s8[6291456]{0:T(1024)(128)(4,1)}), s8[2097152]{0:T(1024)(128)(4,1)S(1)}, s32[]{:S(2)}) async-start(s8[6291456]{0:T(1024)(128)(4,1)} %bitcast.198), calls=%async_computation.16 | async-start | bytes 4194304
  214.4 138.6 %copy-start.18 = (bf16[2048,768]{1,0:T(8,128)(2,1)S(1)}, bf16[2048,768]{1,0:T(8,128)(2,1)}, u32[]{:S(2)}) copy-start(bf16[2048,768]{1,0:T(8,128)(2,1)} %param.49) | copy-start | bytes 9437188
  356.7 3.4 copy-start.6
  360.1 3.8 slice-start.8
  364.0 5.4 slice-start.5
  364.0 5.7 slice-start.6
  370.1 7.8 slice-start
  370.1 7.8 slice-start.1
  387.6 3.7 slice-start.10
  387.6 4.0 slice-start.11
  398.0 5.4 copy-start.20
  414.3 3.2 copy-start.14
  416.4 4.6 copy-start.15
  419.9 184.6 %all-reduce.16.cloned.1.call-start = ((), (), s32[]{:S(2)}) async-start(), calls=%async_computation.11 | async-start | bytes 12582912 | tf_op jit(solution)/shard_map/psum | solution.py:117
  428.0 247.5 %reduce-scatter.17.cloned.1.call-start = ((), (), s32[]{:S(2)}) async-start(), calls=%async_computation.8 | async-start | bytes 2211840
  437.1 310.9 %reduce-scatter.13.cloned.1.call-start = ((), (), s32[]{:S(2)}) async-start(), calls=%async_computation.6 | async-start | bytes 2654208 | tf_op jit(solution)/shard_map/reduce_scatter | solution.py:211
  444.0 7.0 copy-start.42
  444.1 376.9 %reduce-scatter.15.cloned.1.call-start = ((), (), s32[]{:S(2)}) async-start(), calls=%async_computation.7 | async-start | bytes 2654208 | tf_op jit(solution)/shard_map/reduce_scatter | solution.py:213
  451.0 158.6 %copy-start.28 = (f32[768]{0:T(1024)S(1)}, f32[768]{0:T(1024)}, u32[]{:S(2)}) copy-start(f32[768]{0:T(1024)} %get-tuple-element.154) | copy-start | bytes 9220
  451.1 158.6 %copy-start.29 = (f32[768]{0:T(1024)S(1)}, f32[768]{0:T(1024)}, u32[]{:S(2)}) copy-start(f32[768]{0:T(1024)} %get-tuple-element.159) | copy-start | bytes 9220
  451.1 158.6 %copy-start.30 = (f32[768]{0:T(1024)S(1)}, f32[768]{0:T(1024)}, u32[]{:S(2)}) copy-start(f32[768]{0:T(1024)} %get-tuple-element.175) | copy-start | bytes 9220
  451.1 158.6 %copy-start.31 = (f32[768]{0:T(1024)S(1)}, f32[768]{0:T(1024)}, u32[]{:S(2)}) copy-start(f32[768]{0:T(1024)} %get-tuple-element.183) | copy-start | bytes 9220
  604.5 53.7 %slice-start.12 = ((s8[6291456]{0:T(1024)(128)(4,1)}), s8[2097152]{0:T(1024)(128)(4,1)S(1)}, s32[]{:S(2)}) async-start(s8[6291456]{0:T(1024)(128)(4,1)} %bitcast.206), calls=%async_computation.24 | async-start | bytes 4194304
  651.7 6.5 slice-start.13
  651.7 6.5 copy-start.8
  651.7 8.0 copy-start.11
  651.8 8.0 copy-start.34
  651.8 169.2 %copy-start.1 = (bf16[768,768]{1,0:T(8,128)(2,1)S(1)}, bf16[768,768]{1,0:T(8,128)(2,1)}, u32[]{:S(2)}) copy-start(bf16[768,768]{1,0:T(8,128)(2,1)} %param.47) | copy-start | bytes 3538948
  (20 other events, 38.2 us)
Sparse Core Ops, SparseCore 0:
  47.7 122.2 all-reduce.13
  207.9 63.3 reduce-scatter.20
  420.0 63.5 reduce-scatter.18
  485.8 118.6 all-reduce.15
  607.8 67.7 reduce-scatter.16
  679.5 68.3 reduce-scatter.12
  752.0 68.9 reduce-scatter.14
